TPU v7x, 512 devices: a whole 4x8x8 slice. The times are simulated.
512 devices in a mesh: section: 16 (over x_hi, y), fsdp: 32 (over x_lo, z, core).
Axes of the slice: x: 4 (x_hi: 2, x_lo: 2; x = x_hi * 2 + x_lo), y: 8, z: 8, core: 2. Of those that a mesh axis runs over, the one named last changes fastest.
Arguments:
- inputs: bfloat16 [16, 8, 1024, 4096], P('section', None, 'fsdp'), may hold values from -6 to 6
- upstream: bfloat16 [8, 1024, 4096], P(None, 'fsdp'), may hold values from -6 to 6
- weights: bfloat16 [16, 4096, 512], P('section', 'fsdp')
- gain: bfloat16 [16, 4096], P('section', 'fsdp'), may hold values from 0.5 to 1.5
Outputs:
- weight_grad: float32 [16, 4096, 512], P('section', 'fsdp')
- gain_grad: float32 [16, 4096], P('section')
All inputs are finite; a program needn't handle non-finite values.
Results may differ from a plain program's by a relative error of at most 0.035.
Values may be sent and summed in bfloat16 or wider, within the bound.
No kernel may reach another device: no remote copies, remote signals or barrier semaphores. Data moves between devices by JAX's collectives and lax.ppermute only.
A program may use at most 128 MiB of HBM per device.

v0:
```python
import jax
import jax.numpy as jnp
from jax import lax
from jax.sharding import PartitionSpec as P


def passed_along(value, axis, steps):
    count = lax.axis_size(axis)
    leading, last = (max(0, -steps), min(count, count - steps))
    return lax.ppermute(value, axis, [(source, source + steps) for source in range(leading, last)])


def rope_tables(length, head):
    half_head = head // 2
    position = lax.iota(jnp.float32, length)
    freq = jnp.power(500000.0, -2.0 * lax.iota(jnp.float32, half_head) / head)
    angle = position[:, None] * freq[None, :]
    return (jnp.cos(angle), jnp.sin(angle))


def rotate(value_rows, cosine, sine_table):
    half_head = value_rows.shape[-1] // 2
    first = value_rows[..., :half_head]
    second = value_rows[..., half_head:]
    return jnp.concatenate(
        [first * cosine - second * sine_table, second * cosine + first * sine_table], axis=-1
    )


def unrotate(value_rows, cosine, sine_table):
    half_head = value_rows.shape[-1] // 2
    first = value_rows[..., :half_head]
    second = value_rows[..., half_head:]
    return jnp.concatenate(
        [first * cosine + second * sine_table, second * cosine - first * sine_table], axis=-1
    )


def contract_rows(left, right):
    return lax.dot_general(
        left, right, (((0,), (0,)), ((), ())), preferred_element_type=jnp.float32
    )


def contract_cols(left, right):
    return lax.dot_general(
        left, right, (((1,), (1,)), ((), ())), preferred_element_type=jnp.float32
    )


def on_device(inputs, upstream, weights, gain):
    sections = lax.axis_size("section")
    here = lax.axis_index("section")
    micro_count = inputs.shape[1]
    length = inputs.shape[2]
    width = inputs.shape[3]
    head = weights.shape[2] // 4
    tokens_all = micro_count * length
    xfloat = inputs[0].reshape(tokens_all, width).astype(jnp.float32)
    inv_rms = lax.rsqrt(jnp.mean(xfloat * xfloat, axis=1, keepdims=True) + 1e-05)
    normed = xfloat * inv_rms
    w_full, gain_full = (
        lax.all_gather(weights[0], "fsdp", axis=0, tiled=True),
        lax.all_gather(gain[0], "fsdp", axis=0, tiled=True),
    )
    hidden = (normed * gain_full.astype(jnp.float32)).astype(jnp.bfloat16)
    proj = jnp.dot(hidden, w_full[:, : 3 * head], preferred_element_type=jnp.float32)
    wide_gain = gain_full.astype(jnp.float32)
    w_proj = w_full[:, : 3 * head]
    w_back = w_full[:, 3 * head :]
    cosine, sine_table = rope_tables(length, head)
    proj_seq = proj.reshape(micro_count, length, 3 * head)
    query_rows = rotate(proj_seq[..., :head], cosine, sine_table).astype(jnp.bfloat16)
    key_rows = rotate(proj_seq[..., head : 2 * head], cosine, sine_table).astype(jnp.bfloat16)
    value_rows = proj_seq[..., 2 * head :].astype(jnp.bfloat16)
    score_scale = head ** (-0.5)
    causal = lax.broadcasted_iota(jnp.int32, (length, length), 0) >= lax.broadcasted_iota(
        jnp.int32, (length, length), 1
    )

    def work(micro, grad_in, state):
        grad_store, proj_store, att_store, gain_acc, extra = state
        query_m = lax.dynamic_index_in_dim(query_rows, micro, 0, keepdims=False)
        keys_m = lax.dynamic_index_in_dim(key_rows, micro, 0, keepdims=False)
        values_m = lax.dynamic_index_in_dim(value_rows, micro, 0, keepdims=False)
        normed_m = lax.dynamic_slice_in_dim(normed, micro * length, length, 0)
        inv_m = lax.dynamic_slice_in_dim(inv_rms, micro * length, length, 0)
        score_matrix = contract_cols(query_m, keys_m) * score_scale
        probs = jax.nn.softmax(jnp.where(causal, score_matrix, -1e30), axis=-1)
        probability_matrix = probs.astype(jnp.bfloat16)
        attended_output = jnp.dot(
            probability_matrix, values_m, preferred_element_type=jnp.float32
        ).astype(jnp.bfloat16)
        attention_gradient = jnp.dot(grad_in, w_back, preferred_element_type=jnp.float32).astype(
            jnp.bfloat16
        )
        probability_gradient = contract_cols(attention_gradient, values_m)
        score_gradient = (
            probs
            * (probability_gradient - jnp.sum(probability_gradient * probs, axis=-1, keepdims=True))
            * score_scale
        ).astype(jnp.bfloat16)
        query_gradient = jnp.dot(score_gradient, keys_m, preferred_element_type=jnp.float32)
        key_gradient = contract_rows(score_gradient, query_m)
        value_gradient = contract_rows(probability_matrix, attention_gradient)
        grad_proj = jnp.concatenate(
            [
                unrotate(query_gradient, cosine, sine_table),
                unrotate(key_gradient, cosine, sine_table),
                value_gradient,
            ],
            axis=-1,
        ).astype(jnp.bfloat16)
        grad_hidden = contract_cols(grad_proj, w_proj)
        gain_term = jnp.sum(grad_hidden * normed_m, axis=0)
        grad_normed = grad_hidden * wide_gain
        grad_x = inv_m * (
            grad_normed - normed_m * jnp.mean(grad_normed * normed_m, axis=-1, keepdims=True)
        )
        grad_out = (grad_in.astype(jnp.float32) + grad_x).astype(jnp.bfloat16)
        grad_store = lax.dynamic_update_index_in_dim(grad_store, grad_in, micro, 0)
        proj_store = lax.dynamic_update_index_in_dim(proj_store, grad_proj, micro, 0)
        att_store = lax.dynamic_update_index_in_dim(att_store, attended_output, micro, 0)
        return (grad_out, (grad_store, proj_store, att_store, gain_acc + gain_term, extra))

    def spare(micro, grad_in, state):
        return (jnp.zeros_like(grad_in), state)

    def tick(tick_no, received, state):
        micro = tick_no - (sections - 1 - here)
        active = jnp.logical_and(micro >= 0, micro < micro_count)
        clipped = jnp.clip(micro, 0, micro_count - 1)
        top_grad = lax.dynamic_index_in_dim(upstream, clipped, 0, keepdims=False)
        grad_in = jnp.where(here == sections - 1, top_grad, received)
        return lax.cond(active, work, spare, clipped, grad_in, state)

    def step_loop(tick_no, carry):
        received, state = carry
        sent, state = tick(tick_no, received, state)
        received = passed_along(sent, "section", -1)
        return (received, state)

    extra_start = jnp.zeros((1,), jnp.float32)
    state_start = (
        jnp.zeros((micro_count, length, width), jnp.bfloat16),
        jnp.zeros((micro_count, length, 3 * head), jnp.bfloat16),
        jnp.zeros((micro_count, length, head), jnp.bfloat16),
        jnp.zeros((width,), jnp.float32),
        extra_start,
    )
    total_ticks = sections + micro_count - 1
    received, state = lax.fori_loop(
        0, total_ticks - 1, step_loop, (jnp.zeros((length, width), jnp.bfloat16), state_start)
    )
    leftover, state = tick(total_ticks - 1, received, state)
    grad_store, proj_store, att_store, gain_acc, extra = state
    gain_sum = lax.psum(gain_acc, "fsdp")
    grad_flat = grad_store.reshape(tokens_all, width)
    proj_flat = proj_store.reshape(tokens_all, 3 * head)
    att_flat = att_store.reshape(tokens_all, head)
    shard = lax.psum_scatter(
        jnp.concatenate(
            [contract_rows(hidden, proj_flat), contract_rows(grad_flat, att_flat)], axis=1
        ).astype(jnp.bfloat16),
        "fsdp",
        scatter_dimension=0,
        tiled=True,
    ).astype(jnp.float32)
    return (shard[None], gain_sum[None])


def solution(mesh):
    return jax.shard_map(
        on_device,
        mesh=mesh,
        in_specs=(
            P("section", None, "fsdp", None),
            P(None, "fsdp", None),
            P("section", "fsdp", None),
            P("section", "fsdp"),
        ),
        out_specs=(P("section", "fsdp", None), P("section", None)),
        check_vma=False,
    )
```

profile of v0, /device:TPU:8, one launch (start us, length us, event | category | flops | bytes accessed | tf_op | source)
XLA Modules:
  0.0 769.8 jit_solution(6606745490900244712)
XLA Ops:
  10.7 40.3 %all-gather = bf16[1,4096]{1,0:T(2,128)(2,1)S(1)} all-gather(bf16[1,128]{1,0:T(2,128)(2,1)} %param.13), channel_id=2, replica_groups=mesh['section'=16,'fsdp'=32] {'fsdp'}, dimensions={1}, use_global_device_ids=true | all-gather | bytes 8448 | tf_op jit(solution)/shard_map/all_gather | solution.py:64
  53.2 2.5 bitcast_multiply_fusion
  55.6 29.3 %all-gather.4.cloned.1.call-done = bf16[1,4096,512]{2,1,0:T(8,128)(2,1)} async-done(((bf16[1,128,512]{2,1,0:T(8,128)(2,1)}), bf16[1,4096,512]{2,1,0:T(8,128)(2,1)}) %all-gather.4.cloned.1.call-update) | async-done | bytes 4194320 | tf_op jit(solution)/shard_map/all_gather | solution.py:63
  84.9 3.4 fusion.70
  94.9 523.2 %while.26 = (s32[]{:T(128)}, bf16[32,4096]{1,0:T(8,128)(2,1)}, bf16[8,32,4096]{2,1,0:T(8,128)(2,1)}, bf16[8,32,384]{2,1,0:T(8,128)(2,1)}, bf16[8,32,128]{2,1,0:T...) while((s32[]{:T(128)}, bf16[32,4096]{1,0:T(8,128)(2,1)}, ...), condition=%wide.region_9.10_spmd.clone.clone.clone, body=%wide.region_1.9_spmd.clone.clone.clone.sunk | while | flops 137564064 | bytes 10755985 | solution.py:152
  95.7 2.6 collective-permute-start
  98.3 8.0 %collective-permute-done = bf16[32,4096]{1,0:T(8,128)(2,1)S(1)} collective-permute-done((bf16[32,4096]{1,0:T(8,128)(2,1)}, bf16[32,4096]{1,0:T(8,128)(2,1)S(1)}, u32[]{:S(2)}, u32[]{:S(2)}) %collective-permute-start) | collective-permute-done | bytes 262176 | tf_op jit(solution)/shard_map/while/body/eval_jaxpr/ppermute | solution.py:10
  107.7 2.6 collective-permute-start
  110.3 7.1 collective-permute-done
  118.9 2.6 collective-permute-start
  121.5 7.2 collective-permute-done
  132.2 7.2 collective-permute-done
  142.7 7.5 collective-permute-done
  153.6 7.8 %collective-permute-done = bf16[32,4096]{1,0:T(8,128)(2,1)S(1)} collective-permute-done((bf16[32,4096]{1,0:T(8,128)(2,1)}, bf16[32,4096]{1,0:T(8,128)(2,1)S(1)}, u32[]{:S(2)}, u32[]{:S(2)}) %collective-permute-start) | collective-permute-done | bytes 262176 | tf_op jit(solution)/shard_map/while/body/eval_jaxpr/ppermute | solution.py:10
  164.8 7.8 %collective-permute-done = bf16[32,4096]{1,0:T(8,128)(2,1)S(1)} collective-permute-done((bf16[32,4096]{1,0:T(8,128)(2,1)}, bf16[32,4096]{1,0:T(8,128)(2,1)S(1)}, u32[]{:S(2)}, u32[]{:S(2)}) %collective-permute-start) | collective-permute-done | bytes 262176 | tf_op jit(solution)/shard_map/while/body/eval_jaxpr/ppermute | solution.py:10
  175.9 7.9 %collective-permute-done = bf16[32,4096]{1,0:T(8,128)(2,1)S(1)} collective-permute-done((bf16[32,4096]{1,0:T(8,128)(2,1)}, bf16[32,4096]{1,0:T(8,128)(2,1)S(1)}, u32[]{:S(2)}, u32[]{:S(2)}) %collective-permute-start) | collective-permute-done | bytes 262176 | tf_op jit(solution)/shard_map/while/body/eval_jaxpr/ppermute | solution.py:10
  187.3 7.6 collective-permute-done
  198.3 8.9 %collective-permute-done = bf16[32,4096]{1,0:T(8,128)(2,1)S(1)} collective-permute-done((bf16[32,4096]{1,0:T(8,128)(2,1)}, bf16[32,4096]{1,0:T(8,128)(2,1)S(1)}, u32[]{:S(2)}, u32[]{:S(2)}) %collective-permute-start) | collective-permute-done | bytes 262176 | tf_op jit(solution)/shard_map/while/body/eval_jaxpr/ppermute | solution.py:10
  210.6 10.2 %collective-permute-done = bf16[32,4096]{1,0:T(8,128)(2,1)S(1)} collective-permute-done((bf16[32,4096]{1,0:T(8,128)(2,1)}, bf16[32,4096]{1,0:T(8,128)(2,1)S(1)}, u32[]{:S(2)}, u32[]{:S(2)}) %collective-permute-start) | collective-permute-done | bytes 262176 | tf_op jit(solution)/shard_map/while/body/eval_jaxpr/ppermute | solution.py:10
  224.2 11.6 %collective-permute-done = bf16[32,4096]{1,0:T(8,128)(2,1)S(1)} collective-permute-done((bf16[32,4096]{1,0:T(8,128)(2,1)}, bf16[32,4096]{1,0:T(8,128)(2,1)S(1)}, u32[]{:S(2)}, u32[]{:S(2)}) %collective-permute-start) | collective-permute-done | bytes 262176 | tf_op jit(solution)/shard_map/while/body/eval_jaxpr/ppermute | solution.py:10
  239.3 8.6 %collective-permute-done = bf16[32,4096]{1,0:T(8,128)(2,1)S(1)} collective-permute-done((bf16[32,4096]{1,0:T(8,128)(2,1)}, bf16[32,4096]{1,0:T(8,128)(2,1)S(1)}, u32[]{:S(2)}, u32[]{:S(2)}) %collective-permute-start) | collective-permute-done | bytes 262176 | tf_op jit(solution)/shard_map/while/body/eval_jaxpr/ppermute | solution.py:10
  251.3 158.1 %collective-permute-done = bf16[32,4096]{1,0:T(8,128)(2,1)S(1)} collective-permute-done((bf16[32,4096]{1,0:T(8,128)(2,1)}, bf16[32,4096]{1,0:T(8,128)(2,1)S(1)}, u32[]{:S(2)}, u32[]{:S(2)}) %collective-permute-start) | collective-permute-done | bytes 262176 | tf_op jit(solution)/shard_map/while/body/eval_jaxpr/ppermute | solution.py:10
  410.1 13.6 %conditional.7 = (bf16[32,4096]{1,0:T(8,128)(2,1)}, bf16[8,32,4096]{2,1,0:T(8,128)(2,1)}, bf16[8,32,384]{2,1,0:T(8,128)(2,1)}, bf16[8,32,128]{2,1,0:T(8,128)(2,1)}, f32[4096]{0:T(1024)S(1)}) conditional(s32[]{:T(128)} %convert_element_type.189, (bf16[8,32,4096]{2,1,0:T(8,128)(2,1)}, bf16[8,32,384]{2,1,0:T(8,128)(2,1)}, ...), branch_computations={%region_2.2_spmd, %region_3.8_spmd.clone} | conditional | flops 137562016 | bytes 8641706 | solution.py:135
  417.9 2.2 multiply_reduce_fusion.1
  425.6 10.3 %collective-permute-done = bf16[32,4096]{1,0:T(8,128)(2,1)S(1)} collective-permute-done((bf16[32,4096]{1,0:T(8,128)(2,1)}, bf16[32,4096]{1,0:T(8,128)(2,1)S(1)}, u32[]{:S(2)}, u32[]{:S(2)}) %collective-permute-start) | collective-permute-done | bytes 262176 | tf_op jit(solution)/shard_map/while/body/eval_jaxpr/ppermute | solution.py:10
  436.6 13.6 %conditional.7 = (bf16[32,4096]{1,0:T(8,128)(2,1)}, bf16[8,32,4096]{2,1,0:T(8,128)(2,1)}, bf16[8,32,384]{2,1,0:T(8,128)(2,1)}, bf16[8,32,128]{2,1,0:T(8,128)(2,1)}, f32[4096]{0:T(1024)S(1)}) conditional(s32[]{:T(128)} %convert_element_type.189, (bf16[8,32,4096]{2,1,0:T(8,128)(2,1)}, bf16[8,32,384]{2,1,0:T(8,128)(2,1)}, ...), branch_computations={%region_2.2_spmd, %region_3.8_spmd.clone} | conditional | flops 137562016 | bytes 8641706 | solution.py:135
  452.1 10.2 %collective-permute-done = bf16[32,4096]{1,0:T(8,128)(2,1)S(1)} collective-permute-done((bf16[32,4096]{1,0:T(8,128)(2,1)}, bf16[32,4096]{1,0:T(8,128)(2,1)S(1)}, u32[]{:S(2)}, u32[]{:S(2)}) %collective-permute-start) | collective-permute-done | bytes 262176 | tf_op jit(solution)/shard_map/while/body/eval_jaxpr/ppermute | solution.py:10
  463.0 13.6 %conditional.7 = (bf16[32,4096]{1,0:T(8,128)(2,1)}, bf16[8,32,4096]{2,1,0:T(8,128)(2,1)}, bf16[8,32,384]{2,1,0:T(8,128)(2,1)}, bf16[8,32,128]{2,1,0:T(8,128)(2,1)}, f32[4096]{0:T(1024)S(1)}) conditional(s32[]{:T(128)} %convert_element_type.189, (bf16[8,32,4096]{2,1,0:T(8,128)(2,1)}, bf16[8,32,384]{2,1,0:T(8,128)(2,1)}, ...), branch_computations={%region_2.2_spmd, %region_3.8_spmd.clone} | conditional | flops 137562016 | bytes 8641706 | solution.py:135
  478.6 10.4 %collective-permute-done = bf16[32,4096]{1,0:T(8,128)(2,1)S(1)} collective-permute-done((bf16[32,4096]{1,0:T(8,128)(2,1)}, bf16[32,4096]{1,0:T(8,128)(2,1)S(1)}, u32[]{:S(2)}, u32[]{:S(2)}) %collective-permute-start) | collective-permute-done | bytes 262176 | tf_op jit(solution)/shard_map/while/body/eval_jaxpr/ppermute | solution.py:10
  489.7 13.6 %conditional.7 = (bf16[32,4096]{1,0:T(8,128)(2,1)}, bf16[8,32,4096]{2,1,0:T(8,128)(2,1)}, bf16[8,32,384]{2,1,0:T(8,128)(2,1)}, bf16[8,32,128]{2,1,0:T(8,128)(2,1)}, f32[4096]{0:T(1024)S(1)}) conditional(s32[]{:T(128)} %convert_element_type.189, (bf16[8,32,4096]{2,1,0:T(8,128)(2,1)}, bf16[8,32,384]{2,1,0:T(8,128)(2,1)}, ...), branch_computations={%region_2.2_spmd, %region_3.8_spmd.clone} | conditional | flops 137562016 | bytes 8641706 | solution.py:135
  497.6 2.2 multiply_reduce_fusion.1
  505.2 10.0 %collective-permute-done = bf16[32,4096]{1,0:T(8,128)(2,1)S(1)} collective-permute-done((bf16[32,4096]{1,0:T(8,128)(2,1)}, bf16[32,4096]{1,0:T(8,128)(2,1)S(1)}, u32[]{:S(2)}, u32[]{:S(2)}) %collective-permute-start) | collective-permute-done | bytes 262176 | tf_op jit(solution)/shard_map/while/body/eval_jaxpr/ppermute | solution.py:10
  515.9 13.6 %conditional.7 = (bf16[32,4096]{1,0:T(8,128)(2,1)}, bf16[8,32,4096]{2,1,0:T(8,128)(2,1)}, bf16[8,32,384]{2,1,0:T(8,128)(2,1)}, bf16[8,32,128]{2,1,0:T(8,128)(2,1)}, f32[4096]{0:T(1024)S(1)}) conditional(s32[]{:T(128)} %convert_element_type.189, (bf16[8,32,4096]{2,1,0:T(8,128)(2,1)}, bf16[8,32,384]{2,1,0:T(8,128)(2,1)}, ...), branch_computations={%region_2.2_spmd, %region_3.8_spmd.clone} | conditional | flops 137562016 | bytes 8641706 | solution.py:135
  523.8 2.2 multiply_reduce_fusion.1
  531.5 10.2 %collective-permute-done = bf16[32,4096]{1,0:T(8,128)(2,1)S(1)} collective-permute-done((bf16[32,4096]{1,0:T(8,128)(2,1)}, bf16[32,4096]{1,0:T(8,128)(2,1)S(1)}, u32[]{:S(2)}, u32[]{:S(2)}) %collective-permute-start) | collective-permute-done | bytes 262176 | tf_op jit(solution)/shard_map/while/body/eval_jaxpr/ppermute | solution.py:10
  542.5 13.6 %conditional.7 = (bf16[32,4096]{1,0:T(8,128)(2,1)}, bf16[8,32,4096]{2,1,0:T(8,128)(2,1)}, bf16[8,32,384]{2,1,0:T(8,128)(2,1)}, bf16[8,32,128]{2,1,0:T(8,128)(2,1)}, f32[4096]{0:T(1024)S(1)}) conditional(s32[]{:T(128)} %convert_element_type.189, (bf16[8,32,4096]{2,1,0:T(8,128)(2,1)}, bf16[8,32,384]{2,1,0:T(8,128)(2,1)}, ...), branch_computations={%region_2.2_spmd, %region_3.8_spmd.clone} | conditional | flops 137562016 | bytes 8641706 | solution.py:135
  550.4 2.2 multiply_reduce_fusion.1
  558.0 10.1 %collective-permute-done = bf16[32,4096]{1,0:T(8,128)(2,1)S(1)} collective-permute-done((bf16[32,4096]{1,0:T(8,128)(2,1)}, bf16[32,4096]{1,0:T(8,128)(2,1)S(1)}, u32[]{:S(2)}, u32[]{:S(2)}) %collective-permute-start) | collective-permute-done | bytes 262176 | tf_op jit(solution)/shard_map/while/body/eval_jaxpr/ppermute | solution.py:10
  568.8 13.6 %conditional.7 = (bf16[32,4096]{1,0:T(8,128)(2,1)}, bf16[8,32,4096]{2,1,0:T(8,128)(2,1)}, bf16[8,32,384]{2,1,0:T(8,128)(2,1)}, bf16[8,32,128]{2,1,0:T(8,128)(2,1)}, f32[4096]{0:T(1024)S(1)}) conditional(s32[]{:T(128)} %convert_element_type.189, (bf16[8,32,4096]{2,1,0:T(8,128)(2,1)}, bf16[8,32,384]{2,1,0:T(8,128)(2,1)}, ...), branch_computations={%region_2.2_spmd, %region_3.8_spmd.clone} | conditional | flops 137562016 | bytes 8641706 | solution.py:135
  584.3 10.2 %collective-permute-done = bf16[32,4096]{1,0:T(8,128)(2,1)S(1)} collective-permute-done((bf16[32,4096]{1,0:T(8,128)(2,1)}, bf16[32,4096]{1,0:T(8,128)(2,1)S(1)}, u32[]{:S(2)}, u32[]{:S(2)}) %collective-permute-start) | collective-permute-done | bytes 262176 | tf_op jit(solution)/shard_map/while/body/eval_jaxpr/ppermute | solution.py:10
  595.3 13.6 %conditional.7 = (bf16[32,4096]{1,0:T(8,128)(2,1)}, bf16[8,32,4096]{2,1,0:T(8,128)(2,1)}, bf16[8,32,384]{2,1,0:T(8,128)(2,1)}, bf16[8,32,128]{2,1,0:T(8,128)(2,1)}, f32[4096]{0:T(1024)S(1)}) conditional(s32[]{:T(128)} %convert_element_type.189, (bf16[8,32,4096]{2,1,0:T(8,128)(2,1)}, bf16[8,32,384]{2,1,0:T(8,128)(2,1)}, ...), branch_computations={%region_2.2_spmd, %region_3.8_spmd.clone} | conditional | flops 137562016 | bytes 8641706 | solution.py:135
  603.2 2.2 multiply_reduce_fusion.1
  610.9 6.5 collective-permute-done
  618.1 2.8 convolution_convert_fusion.6
  622.2 2.2 pad_maximum_fusion
  624.5 6.5 copy.8
  631.0 104.5 %psum.7 = f32[1,4096]{1,0:T(1,128)} all-reduce(f32[1,4096]{1,0:T(1,128)S(1)} %bitcast.142), channel_id=1, replica_groups=mesh['section'=16,'fsdp'=32] {'fsdp'}, use_global_device_ids=true, to_apply=%region_17.18 | all-reduce | flops 4096 | bytes 32768 | tf_op jit(solution)/shard_map/psum | solution.py:157
  735.4 25.7 %reduce-scatter.4.cloned.1.call-done = bf16[128,512]{1,0:T(8,128)(2,1)} async-done(((bf16[4096,512]{1,0:T(8,128)(2,1)}), bf16[128,512]{1,0:T(8,128)(2,1)}) %reduce-scatter.4.cloned.1.call-update) | async-done | bytes 131088
  (359 shorter events, 185.1 us)
Async XLA Ops:
  7.2 44.0 %copy-start = (bf16[1,8,32,4096]{3,2,1,0:T(8,128)(2,1)S(1)}, bf16[1,8,32,4096]{3,2,1,0:T(8,128)(2,1)}, u32[]{:S(2)}) copy-start(bf16[1,8,32,4096]{3,2,1,0:T(8,128)(2,1)} %param.10) | copy-start | bytes 6291460
  7.2 77.8 %all-gather.4.cloned.1.call-start = ((), (), s32[]{:S(2)}) async-start(), calls=%async_computation.1 | async-start | bytes 4325376 | tf_op jit(solution)/shard_map/all_gather | solution.py:63
  7.9 753.2 %reduce-scatter.4.cloned.1.call-start = ((), (), s32[]{:S(2)}) async-start(), calls=%async_computation.2 | async-start | bytes 4325376
  51.1 39.3 %copy-start.5 = (f32[32,64]{1,0:T(8,128)}, f32[32,64]{1,0:T(8,128)S(1)}, u32[]{:S(2)}) copy-start(f32[32,64]{1,0:T(8,128)S(1)} %get-tuple-element.1389) | copy-start | bytes 24580
  51.1 39.3 %copy-start.6 = (f32[32,64]{1,0:T(8,128)}, f32[32,64]{1,0:T(8,128)S(1)}, u32[]{:S(2)}) copy-start(f32[32,64]{1,0:T(8,128)S(1)} %get-tuple-element.1390) | copy-start | bytes 24580
  84.9 3.4 copy-start.4
  95.7 10.5 %collective-permute-start = (bf16[32,4096]{1,0:T(8,128)(2,1)}, bf16[32,4096]{1,0:T(8,128)(2,1)S(1)}, u32[]{:S(2)}, u32[]{:S(2)}) collective-permute-start(bf16[32,4096]{1,0:T(8,128)(2,1)} %get-tuple-element.1282), channel_id=1, source_target_pairs={{32,0},{64,32},{96,64},{128,96},{160,128},{192,160},{224,192},{256... | collective-permute-start | bytes 786440 | tf_op jit(solution)/shard_map/while/body/eval_jaxpr/ppermute | solution.py:10
  107.7 9.7 %collective-permute-start = (bf16[32,4096]{1,0:T(8,128)(2,1)}, bf16[32,4096]{1,0:T(8,128)(2,1)S(1)}, u32[]{:S(2)}, u32[]{:S(2)}) collective-permute-start(bf16[32,4096]{1,0:T(8,128)(2,1)} %get-tuple-element.1282), channel_id=1, source_target_pairs={{32,0},{64,32},{96,64},{128,96},{160,128},{192,160},{224,192},{256... | collective-permute-start | bytes 786440 | tf_op jit(solution)/shard_map/while/body/eval_jaxpr/ppermute | solution.py:10
  117.4 0.7 copy-start.2
  118.9 9.8 %collective-permute-start = (bf16[32,4096]{1,0:T(8,128)(2,1)}, bf16[32,4096]{1,0:T(8,128)(2,1)S(1)}, u32[]{:S(2)}, u32[]{:S(2)}) collective-permute-start(bf16[32,4096]{1,0:T(8,128)(2,1)} %get-tuple-element.1282), channel_id=1, source_target_pairs={{32,0},{64,32},{96,64},{128,96},{160,128},{192,160},{224,192},{256... | collective-permute-start | bytes 786440 | tf_op jit(solution)/shard_map/while/body/eval_jaxpr/ppermute | solution.py:10
  128.7 0.7 copy-start.2
  130.2 9.1 %collective-permute-start = (bf16[32,4096]{1,0:T(8,128)(2,1)}, bf16[32,4096]{1,0:T(8,128)(2,1)S(1)}, u32[]{:S(2)}, u32[]{:S(2)}) collective-permute-start(bf16[32,4096]{1,0:T(8,128)(2,1)} %get-tuple-element.1282), channel_id=1, source_target_pairs={{32,0},{64,32},{96,64},{128,96},{160,128},{192,160},{224,192},{256... | collective-permute-start | bytes 786440 | tf_op jit(solution)/shard_map/while/body/eval_jaxpr/ppermute | solution.py:10
  139.3 0.7 copy-start.2
  140.8 9.4 %collective-permute-start = (bf16[32,4096]{1,0:T(8,128)(2,1)}, bf16[32,4096]{1,0:T(8,128)(2,1)S(1)}, u32[]{:S(2)}, u32[]{:S(2)}) collective-permute-start(bf16[32,4096]{1,0:T(8,128)(2,1)} %get-tuple-element.1282), channel_id=1, source_target_pairs={{32,0},{64,32},{96,64},{128,96},{160,128},{192,160},{224,192},{256... | collective-permute-start | bytes 786440 | tf_op jit(solution)/shard_map/while/body/eval_jaxpr/ppermute | solution.py:10
  150.2 0.7 copy-start.2
  151.7 9.7 %collective-permute-start = (bf16[32,4096]{1,0:T(8,128)(2,1)}, bf16[32,4096]{1,0:T(8,128)(2,1)S(1)}, u32[]{:S(2)}, u32[]{:S(2)}) collective-permute-start(bf16[32,4096]{1,0:T(8,128)(2,1)} %get-tuple-element.1282), channel_id=1, source_target_pairs={{32,0},{64,32},{96,64},{128,96},{160,128},{192,160},{224,192},{256... | collective-permute-start | bytes 786440 | tf_op jit(solution)/shard_map/while/body/eval_jaxpr/ppermute | solution.py:10
  162.9 9.7 %collective-permute-start = (bf16[32,4096]{1,0:T(8,128)(2,1)}, bf16[32,4096]{1,0:T(8,128)(2,1)S(1)}, u32[]{:S(2)}, u32[]{:S(2)}) collective-permute-start(bf16[32,4096]{1,0:T(8,128)(2,1)} %get-tuple-element.1282), channel_id=1, source_target_pairs={{32,0},{64,32},{96,64},{128,96},{160,128},{192,160},{224,192},{256... | collective-permute-start | bytes 786440 | tf_op jit(solution)/shard_map/while/body/eval_jaxpr/ppermute | solution.py:10
  172.5 0.7 copy-start.2
  174.0 9.8 %collective-permute-start = (bf16[32,4096]{1,0:T(8,128)(2,1)}, bf16[32,4096]{1,0:T(8,128)(2,1)S(1)}, u32[]{:S(2)}, u32[]{:S(2)}) collective-permute-start(bf16[32,4096]{1,0:T(8,128)(2,1)} %get-tuple-element.1282), channel_id=1, source_target_pairs={{32,0},{64,32},{96,64},{128,96},{160,128},{192,160},{224,192},{256... | collective-permute-start | bytes 786440 | tf_op jit(solution)/shard_map/while/body/eval_jaxpr/ppermute | solution.py:10
  185.3 9.5 %collective-permute-start = (bf16[32,4096]{1,0:T(8,128)(2,1)}, bf16[32,4096]{1,0:T(8,128)(2,1)S(1)}, u32[]{:S(2)}, u32[]{:S(2)}) collective-permute-start(bf16[32,4096]{1,0:T(8,128)(2,1)} %get-tuple-element.1282), channel_id=1, source_target_pairs={{32,0},{64,32},{96,64},{128,96},{160,128},{192,160},{224,192},{256... | collective-permute-start | bytes 786440 | tf_op jit(solution)/shard_map/while/body/eval_jaxpr/ppermute | solution.py:10
  194.8 0.7 copy-start.2
  196.3 10.8 %collective-permute-start = (bf16[32,4096]{1,0:T(8,128)(2,1)}, bf16[32,4096]{1,0:T(8,128)(2,1)S(1)}, u32[]{:S(2)}, u32[]{:S(2)}) collective-permute-start(bf16[32,4096]{1,0:T(8,128)(2,1)} %get-tuple-element.1282), channel_id=1, source_target_pairs={{32,0},{64,32},{96,64},{128,96},{160,128},{192,160},{224,192},{256... | collective-permute-start | bytes 786440 | tf_op jit(solution)/shard_map/while/body/eval_jaxpr/ppermute | solution.py:10
  207.2 0.7 copy-start.2
  208.7 12.2 %collective-permute-start = (bf16[32,4096]{1,0:T(8,128)(2,1)}, bf16[32,4096]{1,0:T(8,128)(2,1)S(1)}, u32[]{:S(2)}, u32[]{:S(2)}) collective-permute-start(bf16[32,4096]{1,0:T(8,128)(2,1)} %get-tuple-element.1282), channel_id=1, source_target_pairs={{32,0},{64,32},{96,64},{128,96},{160,128},{192,160},{224,192},{256... | collective-permute-start | bytes 786440 | tf_op jit(solution)/shard_map/while/body/eval_jaxpr/ppermute | solution.py:10
  220.8 0.7 copy-start.2
  222.3 13.5 %collective-permute-start = (bf16[32,4096]{1,0:T(8,128)(2,1)}, bf16[32,4096]{1,0:T(8,128)(2,1)S(1)}, u32[]{:S(2)}, u32[]{:S(2)}) collective-permute-start(bf16[32,4096]{1,0:T(8,128)(2,1)} %get-tuple-element.1282), channel_id=1, source_target_pairs={{32,0},{64,32},{96,64},{128,96},{160,128},{192,160},{224,192},{256... | collective-permute-start | bytes 786440 | tf_op jit(solution)/shard_map/while/body/eval_jaxpr/ppermute | solution.py:10
  235.8 0.7 copy-start.2
  237.3 10.5 %collective-permute-start = (bf16[32,4096]{1,0:T(8,128)(2,1)}, bf16[32,4096]{1,0:T(8,128)(2,1)S(1)}, u32[]{:S(2)}, u32[]{:S(2)}) collective-permute-start(bf16[32,4096]{1,0:T(8,128)(2,1)} %get-tuple-element.1282), channel_id=1, source_target_pairs={{32,0},{64,32},{96,64},{128,96},{160,128},{192,160},{224,192},{256... | collective-permute-start | bytes 786440 | tf_op jit(solution)/shard_map/while/body/eval_jaxpr/ppermute | solution.py:10
  249.4 160.0 %collective-permute-start = (bf16[32,4096]{1,0:T(8,128)(2,1)}, bf16[32,4096]{1,0:T(8,128)(2,1)S(1)}, u32[]{:S(2)}, u32[]{:S(2)}) collective-permute-start(bf16[32,4096]{1,0:T(8,128)(2,1)} %get-tuple-element.1282), channel_id=1, source_target_pairs={{32,0},{64,32},{96,64},{128,96},{160,128},{192,160},{224,192},{256... | collective-permute-start | bytes 786440 | tf_op jit(solution)/shard_map/while/body/eval_jaxpr/ppermute | solution.py:10
  409.3 0.7 copy-start.2
  412.8 7.4 copy-start.7
  423.7 12.2 %collective-permute-start = (bf16[32,4096]{1,0:T(8,128)(2,1)}, bf16[32,4096]{1,0:T(8,128)(2,1)S(1)}, u32[]{:S(2)}, u32[]{:S(2)}) collective-permute-start(bf16[32,4096]{1,0:T(8,128)(2,1)} %get-tuple-element.1282), channel_id=1, source_target_pairs={{32,0},{64,32},{96,64},{128,96},{160,128},{192,160},{224,192},{256... | collective-permute-start | bytes 786440 | tf_op jit(solution)/shard_map/while/body/eval_jaxpr/ppermute | solution.py:10
  435.8 0.7 copy-start.2
  439.3 7.4 copy-start.7
  450.2 12.1 %collective-permute-start = (bf16[32,4096]{1,0:T(8,128)(2,1)}, bf16[32,4096]{1,0:T(8,128)(2,1)S(1)}, u32[]{:S(2)}, u32[]{:S(2)}) collective-permute-start(bf16[32,4096]{1,0:T(8,128)(2,1)} %get-tuple-element.1282), channel_id=1, source_target_pairs={{32,0},{64,32},{96,64},{128,96},{160,128},{192,160},{224,192},{256... | collective-permute-start | bytes 786440 | tf_op jit(solution)/shard_map/while/body/eval_jaxpr/ppermute | solution.py:10
  465.8 7.4 copy-start.7
  476.6 12.3 %collective-permute-start = (bf16[32,4096]{1,0:T(8,128)(2,1)}, bf16[32,4096]{1,0:T(8,128)(2,1)S(1)}, u32[]{:S(2)}, u32[]{:S(2)}) collective-permute-start(bf16[32,4096]{1,0:T(8,128)(2,1)} %get-tuple-element.1282), channel_id=1, source_target_pairs={{32,0},{64,32},{96,64},{128,96},{160,128},{192,160},{224,192},{256... | collective-permute-start | bytes 786440 | tf_op jit(solution)/shard_map/while/body/eval_jaxpr/ppermute | solution.py:10
  492.4 7.4 copy-start.7
  503.3 11.9 %collective-permute-start = (bf16[32,4096]{1,0:T(8,128)(2,1)}, bf16[32,4096]{1,0:T(8,128)(2,1)S(1)}, u32[]{:S(2)}, u32[]{:S(2)}) collective-permute-start(bf16[32,4096]{1,0:T(8,128)(2,1)} %get-tuple-element.1282), channel_id=1, source_target_pairs={{32,0},{64,32},{96,64},{128,96},{160,128},{192,160},{224,192},{256... | collective-permute-start | bytes 786440 | tf_op jit(solution)/shard_map/while/body/eval_jaxpr/ppermute | solution.py:10
  518.7 7.4 copy-start.7
  529.5 12.2 %collective-permute-start = (bf16[32,4096]{1,0:T(8,128)(2,1)}, bf16[32,4096]{1,0:T(8,128)(2,1)S(1)}, u32[]{:S(2)}, u32[]{:S(2)}) collective-permute-start(bf16[32,4096]{1,0:T(8,128)(2,1)} %get-tuple-element.1282), channel_id=1, source_target_pairs={{32,0},{64,32},{96,64},{128,96},{160,128},{192,160},{224,192},{256... | collective-permute-start | bytes 786440 | tf_op jit(solution)/shard_map/while/body/eval_jaxpr/ppermute | solution.py:10
  545.2 7.4 copy-start.7
  556.1 12.0 %collective-permute-start = (bf16[32,4096]{1,0:T(8,128)(2,1)}, bf16[32,4096]{1,0:T(8,128)(2,1)S(1)}, u32[]{:S(2)}, u32[]{:S(2)}) collective-permute-start(bf16[32,4096]{1,0:T(8,128)(2,1)} %get-tuple-element.1282), channel_id=1, source_target_pairs={{32,0},{64,32},{96,64},{128,96},{160,128},{192,160},{224,192},{256... | collective-permute-start | bytes 786440 | tf_op jit(solution)/shard_map/while/body/eval_jaxpr/ppermute | solution.py:10
  571.5 7.4 copy-start.7
  582.4 12.2 %collective-permute-start = (bf16[32,4096]{1,0:T(8,128)(2,1)}, bf16[32,4096]{1,0:T(8,128)(2,1)S(1)}, u32[]{:S(2)}, u32[]{:S(2)}) collective-permute-start(bf16[32,4096]{1,0:T(8,128)(2,1)} %get-tuple-element.1282), channel_id=1, source_target_pairs={{32,0},{64,32},{96,64},{128,96},{160,128},{192,160},{224,192},{256... | collective-permute-start | bytes 786440 | tf_op jit(solution)/shard_map/while/body/eval_jaxpr/ppermute | solution.py:10
  598.1 7.4 copy-start.7
  608.9 8.5 %collective-permute-start = (bf16[32,4096]{1,0:T(8,128)(2,1)}, bf16[32,4096]{1,0:T(8,128)(2,1)S(1)}, u32[]{:S(2)}, u32[]{:S(2)}) collective-permute-start(bf16[32,4096]{1,0:T(8,128)(2,1)} %get-tuple-element.1282), channel_id=1, source_target_pairs={{32,0},{64,32},{96,64},{128,96},{160,128},{192,160},{224,192},{256... | collective-permute-start | bytes 786440 | tf_op jit(solution)/shard_map/while/body/eval_jaxpr/ppermute | solution.py:10
  618.1 2.8 copy-start.1
  (11 other events, 7.7 us)
Sparse Core Ops, SparseCore 0:
  10.2 74.7 all-gather.3
  631.1 129.9 reduce-scatter.3
where the time goes:
time: 774 us; the launch traced here: 770 us
  waiting for transfers between devices  399 us (52%)
  blocking collectives  145 us (19%)
  matrix products  77.3 us (10%)
  local copies, waits for them, and re-layouts  47.5 us (6%)
  starting transfers between devices  44 us (6%)
  other arithmetic  41.4 us (5%)
  between operations  14.2 us (2%)
    ppermute x22, waiting for transfers between devices, passed_along(): lax.ppermute(value, axis, [(source, source + steps) for source in range(l...  343 us
    psum x1, blocking collectives, on_device(): gain_sum = lax.psum(gain_acc, 'fsdp')  104 us
    ppermute x22, starting transfers between devices, passed_along(): lax.ppermute(value, axis, [(source, source + steps) for source in range(l...  44 us
    all_gather x1, blocking collectives, on_device(): lax.all_gather(gain[0], 'fsdp', axis=0, tiled=True)  40.3 us
    dot_general x24, matrix products, contract_cols(): lax.dot_general(left, right, (((1,), (1,)), ((), ())), preferred_element_...  31.5 us
    all_gather x1, waiting for transfers between devices, on_device(): lax.all_gather(weights[0], 'fsdp', axis=0, tiled=True)  29.3 us
    unnamed x3, waiting for transfers between devices  26.4 us
  transfers between devices with their start and end apart: 24, of which 24 were waited for; matrix products, arithmetic and copies ran while one was open for 1% of the time, Pallas kernels for 0%

commit v1 on v0

--- a/solution.py
+++ b/solution.py
@@ -61,7 +61,9 @@
     normed = xfloat * inv_rms
     w_full, gain_full = (
         lax.all_gather(weights[0], "fsdp", axis=0, tiled=True),
-        lax.all_gather(gain[0], "fsdp", axis=0, tiled=True),
+        jnp.concatenate(
+            lax.all_to_all(jnp.stack([gain[0]] * lax.axis_size("fsdp")), "fsdp", 0, 0), axis=0
+        ),
     )
     hidden = (normed * gain_full.astype(jnp.float32)).astype(jnp.bfloat16)
     proj = jnp.dot(hidden, w_full[:, : 3 * head], preferred_element_type=jnp.float32)

time: 774 us -> 774 us (level)
  blocking collectives: 145 us -> 105 us
  waiting for transfers between devices: 399 us -> 427 us
  starting transfers between devices: 44 us -> 55.3 us
    all_gather x1 -> x0, blocking collectives: 40.3 us -> none  [on_device(): lax.all_gather(gain[0], 'fsdp', axis=0, tiled=True)]
    all_gather x1, waiting for transfers between devices: 29.3 us -> 53.9 us  [on_device(): lax.all_gather(weights[0], 'fsdp', axis=0, tiled=True)]
    all_to_all x0 -> x1, starting transfers between devices: none -> 11.6 us  [on_device(): lax.all_to_all(jnp.stack([gain[0]] * lax.axis_size('fsdp')), 'fsdp', 0, 0)]
  transfers between devices with their start and end apart: 24 -> 25, of which waited for: 24 -> 25; matrix products, arithmetic and copies ran while one was open for 1% -> 1% of each run, Pallas kernels for 0% -> 0%
where the time goes in v1:
time: 774 us; the launch traced here: 770 us
  waiting for transfers between devices  427 us (55%)
  blocking collectives  105 us (14%)
  matrix products  77.3 us (10%)
  starting transfers between devices  55.3 us (7%)
  local copies, waits for them, and re-layouts  48.9 us (6%)
  other arithmetic  41.4 us (5%)
  between operations  14.2 us (2%)
    ppermute x22, waiting for transfers between devices, passed_along(): lax.ppermute(value, axis, [(source, source + steps) for source in range(l...  344 us
    psum x1, blocking collectives, on_device(): gain_sum = lax.psum(gain_acc, 'fsdp')  105 us
    all_gather x1, waiting for transfers between devices, on_device(): lax.all_gather(weights[0], 'fsdp', axis=0, tiled=True)  53.9 us
    ppermute x22, starting transfers between devices, passed_along(): lax.ppermute(value, axis, [(source, source + steps) for source in range(l...  43.6 us
    dot_general x24, matrix products, contract_cols(): lax.dot_general(left, right, (((1,), (1,)), ((), ())), preferred_element_...  31.5 us
    unnamed x3, waiting for transfers between devices  26.4 us
  transfers between devices with their start and end apart: 25, of which 25 were waited for; matrix products, arithmetic and copies ran while one was open for 1% of the time, Pallas kernels for 0%

profile of v1, /device:TPU:8, one launch (start us, length us, event | category | flops | bytes accessed | tf_op | source)
XLA Modules:
  0.0 770.1 jit_solution(1975130266579173879)
XLA Ops:
  9.2 11.6 %all-to-all-start = ((bf16[32,1,128]{2,1,0:T(2,128)(2,1)}), bf16[32,1,128]{2,1,0:T(2,128)(2,1)S(1)}, u32[]{:S(2)}, u32[]{:S(2)}) async-start(bf16[32,1,128]{2,1,0:T(2,128)(2,1)} %stack.3), calls=%async_computation | async-start | bytes 32768 | tf_op jit(solution)/shard_map/all_to_all | solution.py:65
  23.1 2.5 bitcast_multiply_fusion
  26.3 2.9 all-to-all-done
  31.2 53.9 %all-gather.3.cloned.1.call-done = bf16[1,4096,512]{2,1,0:T(8,128)(2,1)} async-done(((bf16[1,128,512]{2,1,0:T(8,128)(2,1)}), bf16[1,4096,512]{2,1,0:T(8,128)(2,1)}) %all-gather.3.cloned.1.call-update) | async-done | bytes 4194320 | tf_op jit(solution)/shard_map/all_gather | solution.py:63
  85.1 3.4 fusion.70
  95.0 523.2 %while.26 = (s32[]{:T(128)}, bf16[32,4096]{1,0:T(8,128)(2,1)}, bf16[8,32,4096]{2,1,0:T(8,128)(2,1)}, bf16[8,32,384]{2,1,0:T(8,128)(2,1)}, bf16[8,32,128]{2,1,0:T...) while((s32[]{:T(128)}, bf16[32,4096]{1,0:T(8,128)(2,1)}, ...), condition=%wide.region_9.10_spmd.clone.clone.clone, body=%wide.region_1.9_spmd.clone.clone.clone.sunk | while | flops 137564064 | bytes 10755985 | solution.py:154
  95.8 2.4 collective-permute-start
  98.3 8.1 %collective-permute-done = bf16[32,4096]{1,0:T(8,128)(2,1)S(1)} collective-permute-done((bf16[32,4096]{1,0:T(8,128)(2,1)}, bf16[32,4096]{1,0:T(8,128)(2,1)S(1)}, u32[]{:S(2)}, u32[]{:S(2)}) %collective-permute-start) | collective-permute-done | bytes 262176 | tf_op jit(solution)/shard_map/while/body/eval_jaxpr/ppermute | solution.py:10
  107.8 2.4 collective-permute-start
  110.3 7.3 collective-permute-done
  119.0 2.4 collective-permute-start
  121.5 7.4 collective-permute-done
  132.3 7.2 collective-permute-done
  142.8 7.5 collective-permute-done
  153.7 7.8 %collective-permute-done = bf16[32,4096]{1,0:T(8,128)(2,1)S(1)} collective-permute-done((bf16[32,4096]{1,0:T(8,128)(2,1)}, bf16[32,4096]{1,0:T(8,128)(2,1)S(1)}, u32[]{:S(2)}, u32[]{:S(2)}) %collective-permute-start) | collective-permute-done | bytes 262176 | tf_op jit(solution)/shard_map/while/body/eval_jaxpr/ppermute | solution.py:10
  164.9 7.8 %collective-permute-done = bf16[32,4096]{1,0:T(8,128)(2,1)S(1)} collective-permute-done((bf16[32,4096]{1,0:T(8,128)(2,1)}, bf16[32,4096]{1,0:T(8,128)(2,1)S(1)}, u32[]{:S(2)}, u32[]{:S(2)}) %collective-permute-start) | collective-permute-done | bytes 262176 | tf_op jit(solution)/shard_map/while/body/eval_jaxpr/ppermute | solution.py:10
  176.0 7.9 %collective-permute-done = bf16[32,4096]{1,0:T(8,128)(2,1)S(1)} collective-permute-done((bf16[32,4096]{1,0:T(8,128)(2,1)}, bf16[32,4096]{1,0:T(8,128)(2,1)S(1)}, u32[]{:S(2)}, u32[]{:S(2)}) %collective-permute-start) | collective-permute-done | bytes 262176 | tf_op jit(solution)/shard_map/while/body/eval_jaxpr/ppermute | solution.py:10
  187.4 7.6 collective-permute-done
  198.4 8.9 %collective-permute-done = bf16[32,4096]{1,0:T(8,128)(2,1)S(1)} collective-permute-done((bf16[32,4096]{1,0:T(8,128)(2,1)}, bf16[32,4096]{1,0:T(8,128)(2,1)S(1)}, u32[]{:S(2)}, u32[]{:S(2)}) %collective-permute-start) | collective-permute-done | bytes 262176 | tf_op jit(solution)/shard_map/while/body/eval_jaxpr/ppermute | solution.py:10
  210.7 10.3 %collective-permute-done = bf16[32,4096]{1,0:T(8,128)(2,1)S(1)} collective-permute-done((bf16[32,4096]{1,0:T(8,128)(2,1)}, bf16[32,4096]{1,0:T(8,128)(2,1)S(1)}, u32[]{:S(2)}, u32[]{:S(2)}) %collective-permute-start) | collective-permute-done | bytes 262176 | tf_op jit(solution)/shard_map/while/body/eval_jaxpr/ppermute | solution.py:10
  224.4 11.6 %collective-permute-done = bf16[32,4096]{1,0:T(8,128)(2,1)S(1)} collective-permute-done((bf16[32,4096]{1,0:T(8,128)(2,1)}, bf16[32,4096]{1,0:T(8,128)(2,1)S(1)}, u32[]{:S(2)}, u32[]{:S(2)}) %collective-permute-start) | collective-permute-done | bytes 262176 | tf_op jit(solution)/shard_map/while/body/eval_jaxpr/ppermute | solution.py:10
  239.4 8.6 %collective-permute-done = bf16[32,4096]{1,0:T(8,128)(2,1)S(1)} collective-permute-done((bf16[32,4096]{1,0:T(8,128)(2,1)}, bf16[32,4096]{1,0:T(8,128)(2,1)S(1)}, u32[]{:S(2)}, u32[]{:S(2)}) %collective-permute-start) | collective-permute-done | bytes 262176 | tf_op jit(solution)/shard_map/while/body/eval_jaxpr/ppermute | solution.py:10
  251.4 158.1 %collective-permute-done = bf16[32,4096]{1,0:T(8,128)(2,1)S(1)} collective-permute-done((bf16[32,4096]{1,0:T(8,128)(2,1)}, bf16[32,4096]{1,0:T(8,128)(2,1)S(1)}, u32[]{:S(2)}, u32[]{:S(2)}) %collective-permute-start) | collective-permute-done | bytes 262176 | tf_op jit(solution)/shard_map/while/body/eval_jaxpr/ppermute | solution.py:10
  410.3 13.6 %conditional.7 = (bf16[32,4096]{1,0:T(8,128)(2,1)}, bf16[8,32,4096]{2,1,0:T(8,128)(2,1)}, bf16[8,32,384]{2,1,0:T(8,128)(2,1)}, bf16[8,32,128]{2,1,0:T(8,128)(2,1)}, f32[4096]{0:T(1024)S(1)}) conditional(s32[]{:T(128)} %convert_element_type.197, (bf16[8,32,4096]{2,1,0:T(8,128)(2,1)}, bf16[8,32,384]{2,1,0:T(8,128)(2,1)}, ...), branch_computations={%region_2.2_spmd, %region_3.8_spmd.clone} | conditional | flops 137562016 | bytes 8641706 | solution.py:137
  418.1 2.2 multiply_reduce_fusion.1
  425.8 10.3 %collective-permute-done = bf16[32,4096]{1,0:T(8,128)(2,1)S(1)} collective-permute-done((bf16[32,4096]{1,0:T(8,128)(2,1)}, bf16[32,4096]{1,0:T(8,128)(2,1)S(1)}, u32[]{:S(2)}, u32[]{:S(2)}) %collective-permute-start) | collective-permute-done | bytes 262176 | tf_op jit(solution)/shard_map/while/body/eval_jaxpr/ppermute | solution.py:10
  436.8 13.6 %conditional.7 = (bf16[32,4096]{1,0:T(8,128)(2,1)}, bf16[8,32,4096]{2,1,0:T(8,128)(2,1)}, bf16[8,32,384]{2,1,0:T(8,128)(2,1)}, bf16[8,32,128]{2,1,0:T(8,128)(2,1)}, f32[4096]{0:T(1024)S(1)}) conditional(s32[]{:T(128)} %convert_element_type.197, (bf16[8,32,4096]{2,1,0:T(8,128)(2,1)}, bf16[8,32,384]{2,1,0:T(8,128)(2,1)}, ...), branch_computations={%region_2.2_spmd, %region_3.8_spmd.clone} | conditional | flops 137562016 | bytes 8641706 | solution.py:137
  444.6 2.2 multiply_reduce_fusion.1
  452.3 10.2 %collective-permute-done = bf16[32,4096]{1,0:T(8,128)(2,1)S(1)} collective-permute-done((bf16[32,4096]{1,0:T(8,128)(2,1)}, bf16[32,4096]{1,0:T(8,128)(2,1)S(1)}, u32[]{:S(2)}, u32[]{:S(2)}) %collective-permute-start) | collective-permute-done | bytes 262176 | tf_op jit(solution)/shard_map/while/body/eval_jaxpr/ppermute | solution.py:10
  463.2 13.6 %conditional.7 = (bf16[32,4096]{1,0:T(8,128)(2,1)}, bf16[8,32,4096]{2,1,0:T(8,128)(2,1)}, bf16[8,32,384]{2,1,0:T(8,128)(2,1)}, bf16[8,32,128]{2,1,0:T(8,128)(2,1)}, f32[4096]{0:T(1024)S(1)}) conditional(s32[]{:T(128)} %convert_element_type.197, (bf16[8,32,4096]{2,1,0:T(8,128)(2,1)}, bf16[8,32,384]{2,1,0:T(8,128)(2,1)}, ...), branch_computations={%region_2.2_spmd, %region_3.8_spmd.clone} | conditional | flops 137562016 | bytes 8641706 | solution.py:137
  478.7 10.4 %collective-permute-done = bf16[32,4096]{1,0:T(8,128)(2,1)S(1)} collective-permute-done((bf16[32,4096]{1,0:T(8,128)(2,1)}, bf16[32,4096]{1,0:T(8,128)(2,1)S(1)}, u32[]{:S(2)}, u32[]{:S(2)}) %collective-permute-start) | collective-permute-done | bytes 262176 | tf_op jit(solution)/shard_map/while/body/eval_jaxpr/ppermute | solution.py:10
  489.8 13.6 %conditional.7 = (bf16[32,4096]{1,0:T(8,128)(2,1)}, bf16[8,32,4096]{2,1,0:T(8,128)(2,1)}, bf16[8,32,384]{2,1,0:T(8,128)(2,1)}, bf16[8,32,128]{2,1,0:T(8,128)(2,1)}, f32[4096]{0:T(1024)S(1)}) conditional(s32[]{:T(128)} %convert_element_type.197, (bf16[8,32,4096]{2,1,0:T(8,128)(2,1)}, bf16[8,32,384]{2,1,0:T(8,128)(2,1)}, ...), branch_computations={%region_2.2_spmd, %region_3.8_spmd.clone} | conditional | flops 137562016 | bytes 8641706 | solution.py:137
  505.4 10.0 %collective-permute-done = bf16[32,4096]{1,0:T(8,128)(2,1)S(1)} collective-permute-done((bf16[32,4096]{1,0:T(8,128)(2,1)}, bf16[32,4096]{1,0:T(8,128)(2,1)S(1)}, u32[]{:S(2)}, u32[]{:S(2)}) %collective-permute-start) | collective-permute-done | bytes 262176 | tf_op jit(solution)/shard_map/while/body/eval_jaxpr/ppermute | solution.py:10
  516.1 13.6 %conditional.7 = (bf16[32,4096]{1,0:T(8,128)(2,1)}, bf16[8,32,4096]{2,1,0:T(8,128)(2,1)}, bf16[8,32,384]{2,1,0:T(8,128)(2,1)}, bf16[8,32,128]{2,1,0:T(8,128)(2,1)}, f32[4096]{0:T(1024)S(1)}) conditional(s32[]{:T(128)} %convert_element_type.197, (bf16[8,32,4096]{2,1,0:T(8,128)(2,1)}, bf16[8,32,384]{2,1,0:T(8,128)(2,1)}, ...), branch_computations={%region_2.2_spmd, %region_3.8_spmd.clone} | conditional | flops 137562016 | bytes 8641706 | solution.py:137
  524.0 2.2 multiply_reduce_fusion.1
  531.6 10.2 %collective-permute-done = bf16[32,4096]{1,0:T(8,128)(2,1)S(1)} collective-permute-done((bf16[32,4096]{1,0:T(8,128)(2,1)}, bf16[32,4096]{1,0:T(8,128)(2,1)S(1)}, u32[]{:S(2)}, u32[]{:S(2)}) %collective-permute-start) | collective-permute-done | bytes 262176 | tf_op jit(solution)/shard_map/while/body/eval_jaxpr/ppermute | solution.py:10
  542.6 13.6 %conditional.7 = (bf16[32,4096]{1,0:T(8,128)(2,1)}, bf16[8,32,4096]{2,1,0:T(8,128)(2,1)}, bf16[8,32,384]{2,1,0:T(8,128)(2,1)}, bf16[8,32,128]{2,1,0:T(8,128)(2,1)}, f32[4096]{0:T(1024)S(1)}) conditional(s32[]{:T(128)} %convert_element_type.197, (bf16[8,32,4096]{2,1,0:T(8,128)(2,1)}, bf16[8,32,384]{2,1,0:T(8,128)(2,1)}, ...), branch_computations={%region_2.2_spmd, %region_3.8_spmd.clone} | conditional | flops 137562016 | bytes 8641706 | solution.py:137
  550.5 2.2 multiply_reduce_fusion.1
  558.2 10.1 %collective-permute-done = bf16[32,4096]{1,0:T(8,128)(2,1)S(1)} collective-permute-done((bf16[32,4096]{1,0:T(8,128)(2,1)}, bf16[32,4096]{1,0:T(8,128)(2,1)S(1)}, u32[]{:S(2)}, u32[]{:S(2)}) %collective-permute-start) | collective-permute-done | bytes 262176 | tf_op jit(solution)/shard_map/while/body/eval_jaxpr/ppermute | solution.py:10
  569.0 13.6 %conditional.7 = (bf16[32,4096]{1,0:T(8,128)(2,1)}, bf16[8,32,4096]{2,1,0:T(8,128)(2,1)}, bf16[8,32,384]{2,1,0:T(8,128)(2,1)}, bf16[8,32,128]{2,1,0:T(8,128)(2,1)}, f32[4096]{0:T(1024)S(1)}) conditional(s32[]{:T(128)} %convert_element_type.197, (bf16[8,32,4096]{2,1,0:T(8,128)(2,1)}, bf16[8,32,384]{2,1,0:T(8,128)(2,1)}, ...), branch_computations={%region_2.2_spmd, %region_3.8_spmd.clone} | conditional | flops 137562016 | bytes 8641706 | solution.py:137
  584.5 10.2 %collective-permute-done = bf16[32,4096]{1,0:T(8,128)(2,1)S(1)} collective-permute-done((bf16[32,4096]{1,0:T(8,128)(2,1)}, bf16[32,4096]{1,0:T(8,128)(2,1)S(1)}, u32[]{:S(2)}, u32[]{:S(2)}) %collective-permute-start) | collective-permute-done | bytes 262176 | tf_op jit(solution)/shard_map/while/body/eval_jaxpr/ppermute | solution.py:10
  595.5 13.6 %conditional.7 = (bf16[32,4096]{1,0:T(8,128)(2,1)}, bf16[8,32,4096]{2,1,0:T(8,128)(2,1)}, bf16[8,32,384]{2,1,0:T(8,128)(2,1)}, bf16[8,32,128]{2,1,0:T(8,128)(2,1)}, f32[4096]{0:T(1024)S(1)}) conditional(s32[]{:T(128)} %convert_element_type.197, (bf16[8,32,4096]{2,1,0:T(8,128)(2,1)}, bf16[8,32,384]{2,1,0:T(8,128)(2,1)}, ...), branch_computations={%region_2.2_spmd, %region_3.8_spmd.clone} | conditional | flops 137562016 | bytes 8641706 | solution.py:137
  611.0 6.5 collective-permute-done
  618.3 2.8 convolution_convert_fusion.6
  622.4 2.2 pad_maximum_fusion
  624.6 6.5 copy.8
  631.1 104.5 %psum.7 = f32[1,4096]{1,0:T(1,128)} all-reduce(f32[1,4096]{1,0:T(1,128)S(1)} %bitcast.143), channel_id=1, replica_groups=mesh['section'=16,'fsdp'=32] {'fsdp'}, use_global_device_ids=true, to_apply=%region_17.18 | all-reduce | flops 4096 | bytes 32768 | tf_op jit(solution)/shard_map/psum | solution.py:159
  735.6 25.7 %reduce-scatter.4.cloned.1.call-done = bf16[128,512]{1,0:T(8,128)(2,1)} async-done(((bf16[4096,512]{1,0:T(8,128)(2,1)}), bf16[128,512]{1,0:T(8,128)(2,1)}) %reduce-scatter.4.cloned.1.call-update) | async-done | bytes 131088
  (361 shorter events, 188.6 us)
Async XLA Ops:
  7.2 15.9 %copy-start = (bf16[1,8,32,4096]{3,2,1,0:T(8,128)(2,1)S(1)}, bf16[1,8,32,4096]{3,2,1,0:T(8,128)(2,1)}, u32[]{:S(2)}) copy-start(bf16[1,8,32,4096]{3,2,1,0:T(8,128)(2,1)} %param.10) | copy-start | bytes 6291460
  7.2 77.9 %all-gather.3.cloned.1.call-start = ((), (), s32[]{:S(2)}) async-start(), calls=%async_computation.2 | async-start | bytes 4325376 | tf_op jit(solution)/shard_map/all_gather | solution.py:63
  9.2 20.0 %all-to-all-start = ((bf16[32,1,128]{2,1,0:T(2,128)(2,1)}), bf16[32,1,128]{2,1,0:T(2,128)(2,1)S(1)}, u32[]{:S(2)}, u32[]{:S(2)}) async-start(bf16[32,1,128]{2,1,0:T(2,128)(2,1)} %stack.3), calls=%async_computation | async-start | bytes 32768 | tf_op jit(solution)/shard_map/all_to_all | solution.py:65
  20.8 740.5 %reduce-scatter.4.cloned.1.call-start = ((), (), s32[]{:S(2)}) async-start(), calls=%async_computation.3 | async-start | bytes 4325376
  25.6 64.9 %copy-start.5 = (f32[32,64]{1,0:T(8,128)}, f32[32,64]{1,0:T(8,128)S(1)}, u32[]{:S(2)}) copy-start(f32[32,64]{1,0:T(8,128)S(1)} %get-tuple-element.1389) | copy-start | bytes 24580
  25.6 64.9 %copy-start.6 = (f32[32,64]{1,0:T(8,128)}, f32[32,64]{1,0:T(8,128)S(1)}, u32[]{:S(2)}) copy-start(f32[32,64]{1,0:T(8,128)S(1)} %get-tuple-element.1390) | copy-start | bytes 24580
  85.1 3.4 copy-start.4
  95.8 10.5 %collective-permute-start = (bf16[32,4096]{1,0:T(8,128)(2,1)}, bf16[32,4096]{1,0:T(8,128)(2,1)S(1)}, u32[]{:S(2)}, u32[]{:S(2)}) collective-permute-start(bf16[32,4096]{1,0:T(8,128)(2,1)} %get-tuple-element.1282), channel_id=1, source_target_pairs={{32,0},{64,32},{96,64},{128,96},{160,128},{192,160},{224,192},{256... | collective-permute-start | bytes 786440 | tf_op jit(solution)/shard_map/while/body/eval_jaxpr/ppermute | solution.py:10
  106.4 0.7 copy-start.2
  107.8 9.7 %collective-permute-start = (bf16[32,4096]{1,0:T(8,128)(2,1)}, bf16[32,4096]{1,0:T(8,128)(2,1)S(1)}, u32[]{:S(2)}, u32[]{:S(2)}) collective-permute-start(bf16[32,4096]{1,0:T(8,128)(2,1)} %get-tuple-element.1282), channel_id=1, source_target_pairs={{32,0},{64,32},{96,64},{128,96},{160,128},{192,160},{224,192},{256... | collective-permute-start | bytes 786440 | tf_op jit(solution)/shard_map/while/body/eval_jaxpr/ppermute | solution.py:10
  117.6 0.7 copy-start.2
  119.0 9.8 %collective-permute-start = (bf16[32,4096]{1,0:T(8,128)(2,1)}, bf16[32,4096]{1,0:T(8,128)(2,1)S(1)}, u32[]{:S(2)}, u32[]{:S(2)}) collective-permute-start(bf16[32,4096]{1,0:T(8,128)(2,1)} %get-tuple-element.1282), channel_id=1, source_target_pairs={{32,0},{64,32},{96,64},{128,96},{160,128},{192,160},{224,192},{256... | collective-permute-start | bytes 786440 | tf_op jit(solution)/shard_map/while/body/eval_jaxpr/ppermute | solution.py:10
  128.9 0.7 copy-start.2
  130.3 9.1 %collective-permute-start = (bf16[32,4096]{1,0:T(8,128)(2,1)}, bf16[32,4096]{1,0:T(8,128)(2,1)S(1)}, u32[]{:S(2)}, u32[]{:S(2)}) collective-permute-start(bf16[32,4096]{1,0:T(8,128)(2,1)} %get-tuple-element.1282), channel_id=1, source_target_pairs={{32,0},{64,32},{96,64},{128,96},{160,128},{192,160},{224,192},{256... | collective-permute-start | bytes 786440 | tf_op jit(solution)/shard_map/while/body/eval_jaxpr/ppermute | solution.py:10
  139.4 0.7 copy-start.2
  140.9 9.4 %collective-permute-start = (bf16[32,4096]{1,0:T(8,128)(2,1)}, bf16[32,4096]{1,0:T(8,128)(2,1)S(1)}, u32[]{:S(2)}, u32[]{:S(2)}) collective-permute-start(bf16[32,4096]{1,0:T(8,128)(2,1)} %get-tuple-element.1282), channel_id=1, source_target_pairs={{32,0},{64,32},{96,64},{128,96},{160,128},{192,160},{224,192},{256... | collective-permute-start | bytes 786440 | tf_op jit(solution)/shard_map/while/body/eval_jaxpr/ppermute | solution.py:10
  150.3 0.7 copy-start.2
  151.8 9.7 %collective-permute-start = (bf16[32,4096]{1,0:T(8,128)(2,1)}, bf16[32,4096]{1,0:T(8,128)(2,1)S(1)}, u32[]{:S(2)}, u32[]{:S(2)}) collective-permute-start(bf16[32,4096]{1,0:T(8,128)(2,1)} %get-tuple-element.1282), channel_id=1, source_target_pairs={{32,0},{64,32},{96,64},{128,96},{160,128},{192,160},{224,192},{256... | collective-permute-start | bytes 786440 | tf_op jit(solution)/shard_map/while/body/eval_jaxpr/ppermute | solution.py:10
  161.5 0.7 copy-start.2
  163.0 9.7 %collective-permute-start = (bf16[32,4096]{1,0:T(8,128)(2,1)}, bf16[32,4096]{1,0:T(8,128)(2,1)S(1)}, u32[]{:S(2)}, u32[]{:S(2)}) collective-permute-start(bf16[32,4096]{1,0:T(8,128)(2,1)} %get-tuple-element.1282), channel_id=1, source_target_pairs={{32,0},{64,32},{96,64},{128,96},{160,128},{192,160},{224,192},{256... | collective-permute-start | bytes 786440 | tf_op jit(solution)/shard_map/while/body/eval_jaxpr/ppermute | solution.py:10
  172.6 0.7 copy-start.2
  174.1 9.8 %collective-permute-start = (bf16[32,4096]{1,0:T(8,128)(2,1)}, bf16[32,4096]{1,0:T(8,128)(2,1)S(1)}, u32[]{:S(2)}, u32[]{:S(2)}) collective-permute-start(bf16[32,4096]{1,0:T(8,128)(2,1)} %get-tuple-element.1282), channel_id=1, source_target_pairs={{32,0},{64,32},{96,64},{128,96},{160,128},{192,160},{224,192},{256... | collective-permute-start | bytes 786440 | tf_op jit(solution)/shard_map/while/body/eval_jaxpr/ppermute | solution.py:10
  185.5 9.5 %collective-permute-start = (bf16[32,4096]{1,0:T(8,128)(2,1)}, bf16[32,4096]{1,0:T(8,128)(2,1)S(1)}, u32[]{:S(2)}, u32[]{:S(2)}) collective-permute-start(bf16[32,4096]{1,0:T(8,128)(2,1)} %get-tuple-element.1282), channel_id=1, source_target_pairs={{32,0},{64,32},{96,64},{128,96},{160,128},{192,160},{224,192},{256... | collective-permute-start | bytes 786440 | tf_op jit(solution)/shard_map/while/body/eval_jaxpr/ppermute | solution.py:10
  196.4 10.8 %collective-permute-start = (bf16[32,4096]{1,0:T(8,128)(2,1)}, bf16[32,4096]{1,0:T(8,128)(2,1)S(1)}, u32[]{:S(2)}, u32[]{:S(2)}) collective-permute-start(bf16[32,4096]{1,0:T(8,128)(2,1)} %get-tuple-element.1282), channel_id=1, source_target_pairs={{32,0},{64,32},{96,64},{128,96},{160,128},{192,160},{224,192},{256... | collective-permute-start | bytes 786440 | tf_op jit(solution)/shard_map/while/body/eval_jaxpr/ppermute | solution.py:10
  207.3 0.7 copy-start.2
  208.8 12.2 %collective-permute-start = (bf16[32,4096]{1,0:T(8,128)(2,1)}, bf16[32,4096]{1,0:T(8,128)(2,1)S(1)}, u32[]{:S(2)}, u32[]{:S(2)}) collective-permute-start(bf16[32,4096]{1,0:T(8,128)(2,1)} %get-tuple-element.1282), channel_id=1, source_target_pairs={{32,0},{64,32},{96,64},{128,96},{160,128},{192,160},{224,192},{256... | collective-permute-start | bytes 786440 | tf_op jit(solution)/shard_map/while/body/eval_jaxpr/ppermute | solution.py:10
  221.0 0.7 copy-start.2
  222.4 13.5 %collective-permute-start = (bf16[32,4096]{1,0:T(8,128)(2,1)}, bf16[32,4096]{1,0:T(8,128)(2,1)S(1)}, u32[]{:S(2)}, u32[]{:S(2)}) collective-permute-start(bf16[32,4096]{1,0:T(8,128)(2,1)} %get-tuple-element.1282), channel_id=1, source_target_pairs={{32,0},{64,32},{96,64},{128,96},{160,128},{192,160},{224,192},{256... | collective-permute-start | bytes 786440 | tf_op jit(solution)/shard_map/while/body/eval_jaxpr/ppermute | solution.py:10
  237.5 10.5 %collective-permute-start = (bf16[32,4096]{1,0:T(8,128)(2,1)}, bf16[32,4096]{1,0:T(8,128)(2,1)S(1)}, u32[]{:S(2)}, u32[]{:S(2)}) collective-permute-start(bf16[32,4096]{1,0:T(8,128)(2,1)} %get-tuple-element.1282), channel_id=1, source_target_pairs={{32,0},{64,32},{96,64},{128,96},{160,128},{192,160},{224,192},{256... | collective-permute-start | bytes 786440 | tf_op jit(solution)/shard_map/while/body/eval_jaxpr/ppermute | solution.py:10
  249.5 160.0 %collective-permute-start = (bf16[32,4096]{1,0:T(8,128)(2,1)}, bf16[32,4096]{1,0:T(8,128)(2,1)S(1)}, u32[]{:S(2)}, u32[]{:S(2)}) collective-permute-start(bf16[32,4096]{1,0:T(8,128)(2,1)} %get-tuple-element.1282), channel_id=1, source_target_pairs={{32,0},{64,32},{96,64},{128,96},{160,128},{192,160},{224,192},{256... | collective-permute-start | bytes 786440 | tf_op jit(solution)/shard_map/while/body/eval_jaxpr/ppermute | solution.py:10
  409.5 0.7 copy-start.2
  413.0 7.4 copy-start.7
  423.8 12.2 %collective-permute-start = (bf16[32,4096]{1,0:T(8,128)(2,1)}, bf16[32,4096]{1,0:T(8,128)(2,1)S(1)}, u32[]{:S(2)}, u32[]{:S(2)}) collective-permute-start(bf16[32,4096]{1,0:T(8,128)(2,1)} %get-tuple-element.1282), channel_id=1, source_target_pairs={{32,0},{64,32},{96,64},{128,96},{160,128},{192,160},{224,192},{256... | collective-permute-start | bytes 786440 | tf_op jit(solution)/shard_map/while/body/eval_jaxpr/ppermute | solution.py:10
  439.5 7.4 copy-start.7
  450.4 12.1 %collective-permute-start = (bf16[32,4096]{1,0:T(8,128)(2,1)}, bf16[32,4096]{1,0:T(8,128)(2,1)S(1)}, u32[]{:S(2)}, u32[]{:S(2)}) collective-permute-start(bf16[32,4096]{1,0:T(8,128)(2,1)} %get-tuple-element.1282), channel_id=1, source_target_pairs={{32,0},{64,32},{96,64},{128,96},{160,128},{192,160},{224,192},{256... | collective-permute-start | bytes 786440 | tf_op jit(solution)/shard_map/while/body/eval_jaxpr/ppermute | solution.py:10
  465.9 7.4 copy-start.7
  476.8 12.3 %collective-permute-start = (bf16[32,4096]{1,0:T(8,128)(2,1)}, bf16[32,4096]{1,0:T(8,128)(2,1)S(1)}, u32[]{:S(2)}, u32[]{:S(2)}) collective-permute-start(bf16[32,4096]{1,0:T(8,128)(2,1)} %get-tuple-element.1282), channel_id=1, source_target_pairs={{32,0},{64,32},{96,64},{128,96},{160,128},{192,160},{224,192},{256... | collective-permute-start | bytes 786440 | tf_op jit(solution)/shard_map/while/body/eval_jaxpr/ppermute | solution.py:10
  492.6 7.4 copy-start.7
  503.5 11.9 %collective-permute-start = (bf16[32,4096]{1,0:T(8,128)(2,1)}, bf16[32,4096]{1,0:T(8,128)(2,1)S(1)}, u32[]{:S(2)}, u32[]{:S(2)}) collective-permute-start(bf16[32,4096]{1,0:T(8,128)(2,1)} %get-tuple-element.1282), channel_id=1, source_target_pairs={{32,0},{64,32},{96,64},{128,96},{160,128},{192,160},{224,192},{256... | collective-permute-start | bytes 786440 | tf_op jit(solution)/shard_map/while/body/eval_jaxpr/ppermute | solution.py:10
  518.9 7.4 copy-start.7
  529.7 12.2 %collective-permute-start = (bf16[32,4096]{1,0:T(8,128)(2,1)}, bf16[32,4096]{1,0:T(8,128)(2,1)S(1)}, u32[]{:S(2)}, u32[]{:S(2)}) collective-permute-start(bf16[32,4096]{1,0:T(8,128)(2,1)} %get-tuple-element.1282), channel_id=1, source_target_pairs={{32,0},{64,32},{96,64},{128,96},{160,128},{192,160},{224,192},{256... | collective-permute-start | bytes 786440 | tf_op jit(solution)/shard_map/while/body/eval_jaxpr/ppermute | solution.py:10
  545.4 7.4 copy-start.7
  556.3 12.0 %collective-permute-start = (bf16[32,4096]{1,0:T(8,128)(2,1)}, bf16[32,4096]{1,0:T(8,128)(2,1)S(1)}, u32[]{:S(2)}, u32[]{:S(2)}) collective-permute-start(bf16[32,4096]{1,0:T(8,128)(2,1)} %get-tuple-element.1282), channel_id=1, source_target_pairs={{32,0},{64,32},{96,64},{128,96},{160,128},{192,160},{224,192},{256... | collective-permute-start | bytes 786440 | tf_op jit(solution)/shard_map/while/body/eval_jaxpr/ppermute | solution.py:10
  571.7 7.4 copy-start.7
  582.6 12.2 %collective-permute-start = (bf16[32,4096]{1,0:T(8,128)(2,1)}, bf16[32,4096]{1,0:T(8,128)(2,1)S(1)}, u32[]{:S(2)}, u32[]{:S(2)}) collective-permute-start(bf16[32,4096]{1,0:T(8,128)(2,1)} %get-tuple-element.1282), channel_id=1, source_target_pairs={{32,0},{64,32},{96,64},{128,96},{160,128},{192,160},{224,192},{256... | collective-permute-start | bytes 786440 | tf_op jit(solution)/shard_map/while/body/eval_jaxpr/ppermute | solution.py:10
  598.2 7.4 copy-start.7
  609.1 8.5 %collective-permute-start = (bf16[32,4096]{1,0:T(8,128)(2,1)}, bf16[32,4096]{1,0:T(8,128)(2,1)S(1)}, u32[]{:S(2)}, u32[]{:S(2)}) collective-permute-start(bf16[32,4096]{1,0:T(8,128)(2,1)} %get-tuple-element.1282), channel_id=1, source_target_pairs={{32,0},{64,32},{96,64},{128,96},{160,128},{192,160},{224,192},{256... | collective-permute-start | bytes 786440 | tf_op jit(solution)/shard_map/while/body/eval_jaxpr/ppermute | solution.py:10
  618.3 2.8 copy-start.1
  (12 other events, 8.4 us)
Sparse Core Ops, SparseCore 0:
  10.2 74.8 all-gather.2
  631.3 130.0 reduce-scatter.3
